TPU v7x, 128 devices: a whole 4x4x4 slice. The times are simulated.
128 devices in a mesh: tm: 64 (over x, z, y), head: 2 (over core).
Axes of the slice: x: 4, y: 4, z: 4, core: 2. Of those that a mesh axis runs over, the one named last changes fastest.
Arguments:
- series: bfloat16 [16, 65536, 512], P(None, 'tm'), may hold values from -6 to 6
- modes: int32 [128], replicated, may hold values from 1 to 32767, as said below
- query_weight: bfloat16 [512, 512], P(None, 'head'), may hold values from -0.25 to 0.25
- mix_weight: float32 [128, 8, 64, 128], P('tm', 'head'), may hold values from -0.5 to 0.5
- out_weight: bfloat16 [512, 512], P(None, 'head'), may hold values from -0.25 to 0.25
Outputs:
- output: bfloat16 [16, 65536, 512], P(None, 'tm', 'head')
Inputs may be any that keep to these rules, and one draw needn't show every extreme that they name: `modes`: distinct mode numbers; both 1 and one less than half of 65536 are among them.
All inputs are finite; a program needn't handle non-finite values.
Results may differ from a plain program's by a relative error of at most 0.0075.
Values may be sent and summed in bfloat16 or wider, within the bound.
A program may use at most 128 MiB of HBM per device.

v0:
```python
import math
import jax
import jax.numpy as jnp
from jax import lax
from jax.sharding import PartitionSpec as P

two_pi = 2.0 * math.pi


def wave_table(mode_list, first_time, time_count, series_length):
    time_index = first_time + lax.iota(jnp.int32, time_count)
    phases = time_index[:, None] * mode_list[None, :] % series_length
    angles = phases.astype(jnp.float32) * (two_pi / series_length)
    waves = jnp.stack([jnp.cos(angles), -jnp.sin(angles)], axis=2)
    return waves.astype(jnp.bfloat16).reshape(time_count, -1)


def body(series, modes, query_weight, mix_weight, out_weight):
    series_count, shard_rows, model_width = series.shape
    group_width = query_weight.shape[1]
    mode_total = modes.shape[0]
    own_modes, heads_here, head_size, _ = mix_weight.shape
    head_groups = lax.axis_size("head")
    own_series = series_count // head_groups
    series_length = lax.axis_size("tm") * shard_rows
    first_time = lax.axis_index("tm") * shard_rows
    forward_scale = 1.0 / math.sqrt(series_length)
    inverse_scale = 1.0 / math.sqrt(mode_total)
    highest = lax.Precision.HIGHEST
    mine = lax.dynamic_slice_in_dim(series, lax.axis_index("head") * own_series, own_series, 0)
    table = wave_table(modes, first_time, shard_rows, series_length)
    partial = jnp.einsum("tk,btd->kbd", table, mine, preferred_element_type=jnp.float32)
    summed = lax.psum_scatter(partial * forward_scale, "tm", scatter_dimension=0, tiled=True)
    summed = lax.all_gather(summed, "head", axis=1, tiled=True)
    spectrum = jnp.einsum(
        "kbd,df->kbf", summed, query_weight.astype(jnp.float32), precision=highest
    )
    parts = spectrum.reshape(own_modes, 2, series_count, heads_here, head_size)
    from_real = jnp.einsum("mbhi,mhio->mbho", parts[:, 0], mix_weight, precision=highest)
    from_imag = jnp.einsum("mbhi,mhio->mbho", parts[:, 1], mix_weight, precision=highest)
    mixed_real = from_real[..., :head_size] - from_imag[..., head_size:]
    mixed_imag = from_real[..., head_size:] + from_imag[..., :head_size]
    mixed = jnp.stack([mixed_real, mixed_imag], axis=1).astype(jnp.bfloat16)
    mixed = mixed.reshape(2 * own_modes, series_count, group_width)
    mixed = lax.all_gather(mixed, "head", axis=2, tiled=True)
    projected = jnp.einsum("kbf,fo->kbo", mixed, out_weight, preferred_element_type=jnp.float32)
    projected = (projected * inverse_scale).astype(jnp.bfloat16)
    everything = lax.all_gather(projected, "tm", axis=0, tiled=True)
    output = jnp.einsum("tk,kbo->bto", table, everything, preferred_element_type=jnp.float32)
    return output.astype(jnp.bfloat16)


def solution(mesh):
    in_specs = (
        P(None, "tm", None),
        P(),
        P(None, "head"),
        P("tm", "head", None, None),
        P(None, "head"),
    )
    out_specs = P(None, "tm", "head")
    return jax.shard_map(body, mesh=mesh, in_specs=in_specs, out_specs=out_specs, check_vma=False)
```

profile of v0, /device:TPU:0, one launch (start us, length us, event | category | flops | bytes accessed | tf_op | source)
XLA Modules:
  0.0 475.2 jit_solution(6444277786331292956)
XLA Ops:
  6.5 0.0 copy-start
  6.5 0.0 reduce-scatter.2.cloned.1.call-start
  6.5 3.2 cosine_convert_fusion
  9.7 0.1 pad_maximum_fusion
  9.8 0.5 copy.30
  10.3 0.2 reshape.141
  10.5 5.7 %fusion.2 = f32[256,8,512]{2,0,1:T(8,128)S(1)} fusion(bf16[1024,256,1]{0,1,2:T(8,128)(2,1)S(1)} %reshape.141, bf16[16,1024,512]{2,1,0:T(8,128)(2,1)} %param.5, s32[]{:T(128)S(6)} %select_n.22), kind=kOutput, calls=%fused_computation.3 | convolution fusion | flops 2148532224 | bytes 13107204 | tf_op jit(solution)/shard_map/tk,btd->kbd/dot_general | solution.py:32
  16.3 4.4 copy.31
  20.7 0.0 copy-start.1
  20.7 0.0 copy-start.2
  20.7 0.0 reduce-scatter.2.cloned.1.call-update
  20.7 0.0 all-gather.2.cloned.1.call-start
  20.8 360.5 %reduce-scatter.2.cloned.1.call-done = f32[4,8,512]{2,1,0:T(8,128)} async-done(((f32[256,8,512]{2,1,0:T(8,128)}), f32[4,8,512]{2,1,0:T(8,128)}) %reduce-scatter.2.cloned.1.call-update) | async-done | bytes 65552 | tf_op jit(solution)/shard_map/reduce_scatter | solution.py:33
  381.3 0.9 copy.32
  382.2 1.9 all_gather.9
  384.1 0.0 copy-done.1
  384.1 0.3 fusion.12
  384.3 0.1 reshape.140
  384.5 0.0 copy-done
  384.5 0.3 convolution_bitcast_fusion.1
  384.8 0.3 convolution_bitcast_fusion
  385.1 0.1 fusion.17
  385.3 0.1 convert_element_type.36
  385.4 1.8 all_gather.10
  387.3 0.0 copy-done.2
  387.3 0.8 fusion.6
  388.1 0.0 all-gather.2.cloned.1.call-update
  388.1 0.2 convert_element_type.35
  388.3 60.4 %all-gather.2.cloned.1.call-done = bf16[256,16,256]{2,1,0:T(8,128)(2,1)} async-done(((bf16[4,16,256]{2,1,0:T(8,128)(2,1)}), bf16[256,16,256]{2,1,0:T(8,128)(2,1)}) %all-gather.2.cloned.1.call-update) | async-done | bytes 2097168 | tf_op jit(solution)/shard_map/all_gather | solution.py:48
  448.7 7.5 %convert_bitcast_fusion = bf16[16,1024,256]{1,2,0:T(8,128)(2,1)} fusion(bf16[256,16,256]{2,1,0:T(8,128)(2,1)} %all-gather.2.cloned.1.call-done, bf16[1024,256]{0,1:T(8,128)(2,1)S(1)} %convert_element_type.35), kind=kOutput, calls=%fused_computation | convolution fusion | flops 2151677952 | bytes 11010048 | tf_op jit(solution)/shard_map/tk,kbo->bto/dot_general | solution.py:49
  456.2 12.2 %copy.39 = bf16[16,1024,256]{2,1,0:T(8,128)(2,1)} copy(bf16[16,1024,256]{1,2,0:T(8,128)(2,1)} %convert_bitcast_fusion) | data formatting | bytes 16777216 | tf_op jit(solution)/shard_map/convert_element_type | solution.py:50
  (4 shorter events, 0.1 us)
Async XLA Ops:
  6.5 377.9 %copy-start = (f32[2,4,64,128]{3,2,1,0:T(8,128)S(1)}, f32[2,4,64,128]{3,2,1,0:T(8,128)}, u32[]{:S(2)}) copy-start(f32[2,4,64,128]{3,2,1,0:T(8,128)} %param.8) | copy-start | bytes 786436
  6.5 374.7 %reduce-scatter.2.cloned.1.call-start = ((), (), s32[]{:S(2)}) async-start(), calls=%async_computation.1 | async-start | bytes 4259840 | tf_op jit(solution)/shard_map/reduce_scatter | solution.py:33
  20.7 363.4 %copy-start.1 = (bf16[512,256]{1,0:T(8,128)(2,1)S(1)}, bf16[512,256]{1,0:T(8,128)(2,1)}, u32[]{:S(2)}) copy-start(bf16[512,256]{1,0:T(8,128)(2,1)} %param.7) | copy-start | bytes 786436
  20.7 366.6 %copy-start.2 = (bf16[512,256]{1,0:T(8,128)(2,1)S(1)}, bf16[512,256]{1,0:T(8,128)(2,1)}, u32[]{:S(2)}) copy-start(bf16[512,256]{1,0:T(8,128)(2,1)} %param.9) | copy-start | bytes 786436
  20.7 428.0 %all-gather.2.cloned.1.call-start = ((), (), s32[]{:S(2)}) async-start(), calls=%async_computation.2 | async-start | bytes 2129920 | tf_op jit(solution)/shard_map/all_gather | solution.py:48
Sparse Core Ops, SparseCore 0:
  20.9 360.3 reduce-scatter.1
  388.2 60.4 all-gather.1
where the time goes:
time: 476 us; the launch traced here: 475 us
  waiting for transfers between devices  421 us (88%)
  local copies, waits for them, and re-layouts  18.7 us (4%)
  matrix products  14.9 us (3%)
  between operations  13.5 us (3%)
    reduce_scatter x1, waiting for transfers between devices, body(): lax.psum_scatter(partial * forward_scale, 'tm', scatter_dimension=0, tile...  360 us
    all_gather x1, waiting for transfers between devices, body(): everything = lax.all_gather(projected, 'tm', axis=0, tiled=True)  60.4 us
    convert_element_type x1, local copies, waits for them, and re-layouts, body(): return output.astype(jnp.bfloat16)  12.2 us
  transfers between devices with their start and end apart: 2, of which 2 were waited for; matrix products, arithmetic and copies ran while one was open for 0% of the time, Pallas kernels for 0%

commit v1 on v0

--- a/solution.py
+++ b/solution.py
@@ -5,6 +5,11 @@
 from jax.sharding import PartitionSpec as P
 
 two_pi = 2.0 * math.pi
+
+
+def exchange_gather(x, axis, dim):
+    stack = jnp.stack([x] * lax.axis_size(axis))
+    return jnp.concatenate(lax.all_to_all(stack, axis, 0, 0), axis=dim)
 
 
 def wave_table(mode_list, first_time, time_count, series_length):
@@ -45,7 +50,7 @@
     mixed = lax.all_gather(mixed, "head", axis=2, tiled=True)
     projected = jnp.einsum("kbf,fo->kbo", mixed, out_weight, preferred_element_type=jnp.float32)
     projected = (projected * inverse_scale).astype(jnp.bfloat16)
-    everything = lax.all_gather(projected, "tm", axis=0, tiled=True)
+    everything = exchange_gather(projected, "tm", 0)
     output = jnp.einsum("tk,kbo->bto", table, everything, preferred_element_type=jnp.float32)
     return output.astype(jnp.bfloat16)
 

time: 476 us -> 449 us (0.943)
  waiting for transfers between devices: 421 us -> 390 us
    all_gather x1 -> x0, waiting for transfers between devices: 60.4 us -> none  [body(): everything = lax.all_gather(projected, 'tm', axis=0, tiled=True)]
    all_to_all x0 -> x1, waiting for transfers between devices: none -> 29.9 us  [exchange_gather(): return jnp.concatenate(lax.all_to_all(stack, axis, 0, 0), axis=dim)]
where the time goes in v1:
time: 449 us
  waiting for transfers between devices  390 us (87%)
  local copies, waits for them, and re-layouts  20.3 us (5%)
  between operations  13.5 us (3%)
  matrix products  12.8 us (3%)
  starting transfers between devices  4.7 us (1%)
    reduce_scatter x1, waiting for transfers between devices, body(): lax.psum_scatter(partial * forward_scale, 'tm', scatter_dimension=0, tile...  361 us
    all_to_all x1, waiting for transfers between devices, exchange_gather(): return jnp.concatenate(lax.all_to_all(stack, axis, 0, 0), axis=dim)  29.9 us
    convert_element_type x1, local copies, waits for them, and re-layouts, body(): return output.astype(jnp.bfloat16)  12.2 us
  transfers between devices with their start and end apart: 2, of which 2 were waited for; matrix products, arithmetic and copies ran while one was open for 0% of the time, Pallas kernels for 0%

profile of v1, /device:TPU:0, one launch (start us, length us, event | category | flops | bytes accessed | tf_op | source)
XLA Modules:
  0.0 448.9 jit_solution(16668365231518193717)
XLA Ops:
  6.5 0.0 copy-start
  6.5 0.0 reduce-scatter.2.cloned.1.call-start
  6.5 3.2 fusion.14
  9.7 0.1 maximum_convert_fusion
  9.8 0.5 copy.24
  10.3 0.2 reshape.154
  10.5 5.7 %fusion.2 = f32[256,8,512]{2,0,1:T(8,128)S(1)} fusion(bf16[1024,256,1]{0,1,2:T(8,128)(2,1)S(1)} %reshape.154, bf16[16,1024,512]{2,1,0:T(8,128)(2,1)} %param.5, s32[]{:T(128)S(6)} %select_n.22), kind=kOutput, calls=%fused_computation.3 | convolution fusion | flops 2148532224 | bytes 13107204 | tf_op jit(solution)/shard_map/tk,btd->kbd/dot_general | solution.py:37
  16.3 4.4 copy.25
  20.7 0.0 copy-start.1
  20.7 0.0 copy-start.2
  20.7 0.0 reduce-scatter.2.cloned.1.call-update
  20.7 360.5 %reduce-scatter.2.cloned.1.call-done = f32[4,8,512]{2,1,0:T(8,128)} async-done(((f32[256,8,512]{2,1,0:T(8,128)}), f32[4,8,512]{2,1,0:T(8,128)}) %reduce-scatter.2.cloned.1.call-update) | async-done | bytes 65552 | tf_op jit(solution)/shard_map/reduce_scatter | solution.py:38
  381.3 0.9 copy.26
  382.2 1.9 all_gather.6
  384.1 0.0 copy-done.1
  384.1 0.3 fusion.12
  384.3 0.1 reshape.152
  384.5 0.0 copy-done
  384.5 0.3 convolution_bitcast_fusion.1
  384.8 0.3 convolution_bitcast_fusion
  385.1 0.1 fusion.18
  385.3 0.1 convert_element_type.46
  385.4 1.8 all_gather.7
  387.3 0.0 copy-done.2
  387.3 0.2 fusion.6
  387.4 1.6 stack.17
  389.0 4.7 %all-to-all-start = ((bf16[64,4,16,256]{3,2,1,0:T(8,128)(2,1)}), bf16[64,4,16,256]{3,2,1,0:T(8,128)(2,1)S(1)}, u32[]{:S(2)}, u32[]{:S(2)}) async-start(bf16[64,4,16,256]{3,2,1,0:T(8,128)(2,1)} %stack.17), calls=%async_computation.1 | async-start | bytes 4194304 | tf_op jit(solution)/shard_map/all_to_all | solution.py:12
  393.7 0.2 convert_element_type.45
  393.9 29.9 %all-to-all-done = bf16[64,4,16,256]{3,2,1,0:T(8,128)(2,1)S(1)} async-done(((bf16[64,4,16,256]{3,2,1,0:T(8,128)(2,1)}), bf16[64,4,16,256]{3,2,1,0:T(8,128)(2,1)S(1)}, u32[]{:S(2)}, u32[]{:S(2)}) %all-to-all-start) | async-done | bytes 2097184 | tf_op jit(solution)/shard_map/all_to_all | solution.py:12
  423.8 6.0 %convert_bitcast_fusion = bf16[16,1024,256]{1,2,0:T(8,128)(2,1)} fusion(bf16[256,16,256]{2,1,0:T(8,128)(2,1)S(1)} %bitcast.34, bf16[1024,256]{0,1:T(8,128)(2,1)S(1)} %convert_element_type.45), kind=kOutput, calls=%fused_computation | convolution fusion | flops 2151677952 | bytes 11010048 | tf_op jit(solution)/shard_map/tk,kbo->bto/dot_general | solution.py:54
  429.8 12.2 %copy.33 = bf16[16,1024,256]{2,1,0:T(8,128)(2,1)} copy(bf16[16,1024,256]{1,2,0:T(8,128)(2,1)} %convert_bitcast_fusion) | data formatting | bytes 16777216 | tf_op jit(solution)/shard_map/convert_element_type | solution.py:55
  (4 shorter events, 0.1 us)
Async XLA Ops:
  6.5 377.9 %copy-start = (f32[2,4,64,128]{3,2,1,0:T(8,128)S(1)}, f32[2,4,64,128]{3,2,1,0:T(8,128)}, u32[]{:S(2)}) copy-start(f32[2,4,64,128]{3,2,1,0:T(8,128)} %param.8) | copy-start | bytes 786436
  6.5 374.7 %reduce-scatter.2.cloned.1.call-start = ((), (), s32[]{:S(2)}) async-start(), calls=%async_computation.2 | async-start | bytes 4259840 | tf_op jit(solution)/shard_map/reduce_scatter | solution.py:38
  20.7 363.4 %copy-start.1 = (bf16[512,256]{1,0:T(8,128)(2,1)S(1)}, bf16[512,256]{1,0:T(8,128)(2,1)}, u32[]{:S(2)}) copy-start(bf16[512,256]{1,0:T(8,128)(2,1)} %param.7) | copy-start | bytes 786436
  20.7 366.6 %copy-start.2 = (bf16[512,256]{1,0:T(8,128)(2,1)S(1)}, bf16[512,256]{1,0:T(8,128)(2,1)}, u32[]{:S(2)}) copy-start(bf16[512,256]{1,0:T(8,128)(2,1)} %param.9) | copy-start | bytes 786436
  389.0 34.8 %all-to-all-start = ((bf16[64,4,16,256]{3,2,1,0:T(8,128)(2,1)}), bf16[64,4,16,256]{3,2,1,0:T(8,128)(2,1)S(1)}, u32[]{:S(2)}, u32[]{:S(2)}) async-start(bf16[64,4,16,256]{3,2,1,0:T(8,128)(2,1)} %stack.17), calls=%async_computation.1 | async-start | bytes 4194304 | tf_op jit(solution)/shard_map/all_to_all | solution.py:12
Sparse Core Ops, SparseCore 0:
  20.9 360.3 reduce-scatter.1
